TPU v7x, 512 devices: a whole 4x8x8 slice. The times are simulated.
512 devices in a mesh: lat: 64 (over z, x, core), rad: 8 (over y).
Axes of the slice: x: 4, y: 8, z: 8, core: 2. Of those that a mesh axis runs over, the one named last changes fastest.
Arguments:
- fourier: bfloat16 [2, 2, 256, 2, 64, 1152], P(None, None, 'rad', None, None, 'lat'), may hold values from -6 to 6
- legendre: bfloat16 [64, 1024, 1152], P('lat'), may hold values from -0.1875 to 0.1875
- inverse: bfloat16 [1024, 512, 512], P('lat', 'rad'), may hold values from -0.25 to 0.25
- order_of_slot: int32 [64], replicated, may hold values from 0 to 63, each once
- degree_of_slot: int32 [1024], replicated, may hold values from 0 to 1023, each once
- degree_count: int32 [64], replicated, may hold values from 1 to 1024, as said below
Outputs:
- solved: float32 [1024, 512, 2, 64], P('lat', 'rad')
Inputs may be any that keep to these rules, and one draw needn't show every extreme that they name: `order_of_slot`: a permutation; the index p of lat is given slot p. `degree_of_slot`: a permutation; the index p of lat is given slots p * 16 to (p + 1) * 16 - 1. Order k is live on the last degree_count[k] degrees of the band; some order has all 1024.
All inputs are finite; a program needn't handle non-finite values.
Results may differ from a plain program's by a relative error of at most 0.0042.
Values may be sent and summed in bfloat16 or wider, within the bound.
A program may use at most 64 MiB of HBM per device.

v0:
```python
import jax
import jax.numpy as jnp
from jax import lax
from jax.sharding import PartitionSpec as P


def analyze(received, legendre, first_live):
    north_rows = received[:, :, :, 0].astype(jnp.float32)
    south_rows = received[:, :, :, 1].astype(jnp.float32)
    even_part = (north_rows + south_rows).astype(jnp.bfloat16)
    odd_part = (north_rows - south_rows).astype(jnp.bfloat16)
    slot_count = legendre.shape[0]
    band_size = legendre.shape[1]
    band_index = lax.broadcasted_iota(jnp.int32, (slot_count, band_size), 1)
    live_mask = band_index >= first_live[:, None]
    use_even = (band_index - first_live[:, None]) % 2 == 0
    full_even = jnp.einsum(
        "ojn,fcron->ojfcr", legendre, even_part, preferred_element_type=jnp.float32
    )
    full_odd = jnp.einsum(
        "ojn,fcron->ojfcr", legendre, odd_part, preferred_element_type=jnp.float32
    )
    chosen = jnp.where(use_even[:, :, None, None, None], full_even, full_odd)
    return jnp.where(live_mask[:, :, None, None, None], chosen, 0.0).astype(jnp.bfloat16)


def on_device(fourier, legendre, inverse, order_of_slot, degree_of_slot, degree_count):
    slot_count = legendre.shape[0]
    band_size = legendre.shape[1]
    lat_index = lax.axis_index("lat")
    my_orders = lax.dynamic_slice_in_dim(order_of_slot, lat_index * slot_count, slot_count)
    first_live = band_size - jnp.take(degree_count, my_orders)
    picked = jnp.take(fourier, order_of_slot, axis=4)
    received = lax.all_to_all(picked, "lat", split_axis=4, concat_axis=5, tiled=True)
    coefficients = analyze(received, legendre, first_live)
    by_degree = jnp.take(coefficients, degree_of_slot, axis=1)
    at_owner = lax.all_to_all(by_degree, "lat", split_axis=1, concat_axis=0, tiled=True)
    degree_local = inverse.shape[0]
    row_block = inverse.shape[1]
    full_rows = inverse.shape[2]
    matrices = inverse.reshape(degree_local, row_block, 2, full_rows // 2)
    return jnp.einsum(
        "tqfk,mtfck->tqcm",
        matrices,
        lax.all_gather(at_owner, "rad", axis=4, tiled=True),
        preferred_element_type=jnp.float32,
    )


def solution(mesh):
    in_specs = (
        P(None, None, "rad", None, None, "lat"),
        P("lat", None, None),
        P("lat", "rad", None),
        P(),
        P(),
        P(),
    )
    out_specs = P("lat", "rad", None, None)
    return jax.shard_map(
        on_device, mesh=mesh, in_specs=in_specs, out_specs=out_specs, check_vma=False
    )
```

profile of v0, /device:TPU:1, one launch (start us, length us, event | category | flops | bytes accessed | tf_op | source)
XLA Modules:
  0.0 196.2 jit_solution(13776918970840271404)
XLA Ops:
  6.5 0.0 copy-start
  6.5 0.8 compare_select_fusion.1
  7.3 0.7 compare_and_fusion.1
  8.0 7.4 %copy.17 = bf16[2,2,32,2,64,18]{2,5,3,1,0,4:T(8,128)(2,1)} copy(bf16[2,2,32,2,64,18]{4,3,5,2,1,0:T(2,128)(2,1)} %param.6) | data formatting | bytes 1179648 | tf_op args[0]
  15.4 4.5 %gather_fusion = bf16[64,2,2,32,2,18]{3,5,4,2,1,0:T(8,128)(2,1)} fusion(bf16[2,2,32,2,64,18]{2,5,3,1,0,4:T(8,128)(2,1)} %copy.17, s32[1024]{0:T(1024)S(1)} %pad_clamp_fusion), kind=kCustom, calls=%fused_computation | custom fusion | bytes 1179904 | tf_op jit(solution)/shard_map/jit(_take)/gather | solution.py:33
  19.9 2.2 %select_bitcast_fusion = bf16[2,2,32,2,64,18]{2,5,3,1,0,4:T(8,128)(2,1)S(1)} fusion(bf16[64,2,2,32,2,18]{3,5,4,2,1,0:T(8,128)(2,1)} %gather_fusion, pred[64]{0:T(512)(128)(4,1)S(1)} %compare_and_fusion.1), kind=kLoop, calls=%fused_computation.2 | loop fusion | flops 294912 | bytes 1179712 | tf_op jit(solution)/shard_map/jit(_take)/select_n | solution.py:33
  22.2 3.8 %copy.36 = bf16[2,2,32,2,64,18]{2,3,5,1,0,4:T(2,128)(2,1)} copy(bf16[2,2,32,2,64,18]{2,5,3,1,0,4:T(8,128)(2,1)S(1)} %select_bitcast_fusion) | data formatting | bytes 1179648 | tf_op jit(solution)/shard_map/jit(_take)/select_n | solution.py:33
  26.0 6.4 %reshape.148 = bf16[64,2,2304]{2,1,0:T(2,128)(2,1)} reshape(bf16[64,2,2,18,2,32]{5,4,3,2,1,0:T(2,128)(2,1)} %bitcast.59) | data formatting | bytes 1179648
  32.4 14.8 %all-to-all-start = ((bf16[64,2,2304]{2,1,0:T(2,128)(2,1)}), bf16[64,2,2304]{2,1,0:T(2,128)(2,1)S(1)}, u32[]{:S(2)}, u32[]{:S(2)}) async-start(bf16[64,2,2304]{2,1,0:T(2,128)(2,1)} %reshape.148), calls=%async_computation | async-start | bytes 1179648 | tf_op jit(solution)/shard_map/all_to_all | solution.py:34
  47.3 0.2 all-gather.2.cloned.1.call-start
  47.5 0.0 copy-done.2
  47.5 0.6 dynamic_slice.3
  50.0 0.0 copy-done.3
  50.0 0.6 dynamic-slice.2
  51.4 14.9 %all-to-all-done = bf16[64,2,2304]{2,1,0:T(2,128)(2,1)S(1)} async-done(((bf16[64,2,2304]{2,1,0:T(2,128)(2,1)}), bf16[64,2,2304]{2,1,0:T(2,128)(2,1)S(1)}, u32[]{:S(2)}, u32[]{:S(2)}) %all-to-all-start) | async-done | bytes 589856 | tf_op jit(solution)/shard_map/all_to_all | solution.py:34
  66.3 2.4 %reshape.149 = bf16[64,2,2,18,2,32]{5,4,3,2,1,0:T(2,128)(2,1)} reshape(bf16[64,2,2304]{2,1,0:T(2,128)(2,1)S(1)} %all-to-all-done) | data formatting | bytes 1179648
  68.6 10.1 %copy.19 = bf16[2,2,32,2,64,18]{5,4,2,3,1,0:T(8,128)(2,1)} copy(bf16[2,2,32,2,64,18]{2,3,5,1,0,4:T(2,128)(2,1)} %bitcast.58) | data formatting | bytes 1179648 | tf_op jit(solution)/shard_map/all_to_all | solution.py:34
  78.7 7.0 %all_to_all.9 = bf16[2,2,32,2,1,1152]{5,2,3,1,0,4:T(8,128)(2,1)S(1)} reshape(bf16[2,2,32,2,64,18]{5,4,2,3,1,0:T(8,128)(2,1)} %copy.19) | data formatting | bytes 1179648 | tf_op jit(solution)/shard_map/all_to_all | solution.py:34
  85.7 0.9 fusion
  86.6 1.6 fusion.13
  88.2 2.2 %copy.20 = bf16[1024,2,2,32]{3,2,1,0:T(2,128)(2,1)S(1)} copy(bf16[1024,2,2,32]{0,3,2,1:T(8,128)(2,1)} %fusion.13) | data formatting | bytes 524288 | tf_op jit(solution)/shard_map/convert_element_type | solution.py:24
  90.4 8.5 %gather_fusion.1 = bf16[1024,2,2,32]{3,2,1,0:T(2,128)(2,1)} fusion(bf16[1024,2,2,32]{3,2,1,0:T(2,128)(2,1)S(1)} %copy.20, s32[1024]{0:T(1024)S(1)} %fusion.33), kind=kCustom, calls=%fused_computation.1 | custom fusion | bytes 528384 | tf_op jit(solution)/shard_map/jit(_take)/gather | solution.py:36
  98.9 5.3 %fusion.34 = bf16[1024,1,2,2,32]{4,3,2,1,0:T(2,128)(2,1)S(1)} fusion(bf16[1024,2,2,32]{3,2,1,0:T(2,128)(2,1)} %gather_fusion.1, pred[1024]{0:T(1024)(128)(4,1)S(1)} %compare_and_fusion), kind=kLoop, calls=%fused_computation.41 | loop fusion | flops 131072 | bytes 525312
  104.3 1.7 reshape.150
  106.0 18.9 %all_to_all.24 = bf16[64,2,1024]{2,1,0:T(2,128)(2,1)} all-to-all(bf16[64,2,1024]{2,1,0:T(2,128)(2,1)} %reshape.150), channel_id=1, replica_groups=mesh['lat'=64,'rad'=8] {'lat'}, dimensions={0} | all-to-all | bytes 524288 | tf_op jit(solution)/shard_map/all_to_all | solution.py:37
  124.9 3.0 %reshape.151 = bf16[1024,1,2,2,32]{4,3,2,1,0:T(2,128)(2,1)S(1)} reshape(bf16[64,2,1024]{2,1,0:T(2,128)(2,1)} %all_to_all.24) | data formatting | bytes 524288
  128.0 2.2 %copy.23 = bf16[64,16,2,2,32]{0,4,2,3,1:T(8,128)(2,1)} copy(bf16[64,16,2,2,32]{4,3,2,1,0:T(2,128)(2,1)S(1)} %bitcast.60) | data formatting | bytes 524288 | tf_op jit(solution)/shard_map/all_to_all | solution.py:37
  130.1 0.0 all-gather.2.cloned.1.call-update
  130.2 1.3 reshape.96
  131.5 51.1 %all-gather.2.cloned.1.call-done = bf16[64,16,2,2,256]{0,4,2,3,1:T(8,128)(2,1)} async-done(((bf16[64,16,2,2,32]{0,4,2,3,1:T(8,128)(2,1)}), bf16[64,16,2,2,256]{0,4,2,3,1:T(8,128)(2,1)}) %all-gather.2.cloned.1.call-update) | async-done | bytes 2097168 | tf_op jit(solution)/shard_map/all_gather | solution.py:45
  182.6 4.4 %convolution_bitcast_fusion = f32[16,64,2,64]{1,3,2,0:T(8,128)} fusion(bf16[64,16,2,2,256]{0,4,2,3,1:T(8,128)(2,1)} %all-gather.2.cloned.1.call-done, bf16[16,64,2,256,1]{3,2,1,0,4:T(2,128)(2,1)S(1)} %bitcast.61), kind=kOutput, calls=%fused_computation.8 | convolution fusion | flops 134217728 | bytes 3670016 | tf_op jit(solution)/shard_map/tqfk,mtfck->tqcm/dot_general | solution.py:42
  187.1 2.2 %copy.25 = f32[16,64,2,64]{3,2,1,0:T(2,128)} copy(f32[16,64,2,64]{1,3,2,0:T(8,128)} %convolution_bitcast_fusion) | data formatting | bytes 1048576 | tf_op jit(solution)/shard_map/tqfk,mtfck->tqcm/transpose | solution.py:42
  (9 shorter events, 0.0 us)
Async XLA Ops:
  6.5 79.2 %copy-start = (bf16[1,1024,1152]{2,1,0:T(8,128)(2,1)S(1)}, bf16[1,1024,1152]{2,1,0:T(8,128)(2,1)}, u32[]{:S(2)}) copy-start(bf16[1,1024,1152]{2,1,0:T(8,128)(2,1)} %param.7) | copy-start | bytes 7077892
  26.0 21.5 %copy-start.2 = (s32[64]{0:T(128)S(1)}, s32[64]{0:T(128)}, u32[]{:S(2)}) copy-start(s32[64]{0:T(128)} %param.9) | copy-start | bytes 772
  26.0 24.0 %copy-start.3 = (s32[64]{0:T(128)S(1)}, s32[64]{0:T(128)}, u32[]{:S(2)}) copy-start(s32[64]{0:T(128)} %param.11) | copy-start | bytes 772
  26.0 25.3 %copy-start.1 = (s32[1024]{0:T(1024)S(1)}, s32[1024]{0:T(1024)}, u32[]{:S(2)}) copy-start(s32[1024]{0:T(1024)} %param.10) | copy-start | bytes 12292
  32.4 33.8 %all-to-all-start = ((bf16[64,2,2304]{2,1,0:T(2,128)(2,1)}), bf16[64,2,2304]{2,1,0:T(2,128)(2,1)S(1)}, u32[]{:S(2)}, u32[]{:S(2)}) async-start(bf16[64,2,2304]{2,1,0:T(2,128)(2,1)} %reshape.148), calls=%async_computation | async-start | bytes 1179648 | tf_op jit(solution)/shard_map/all_to_all | solution.py:34
  47.3 135.4 %all-gather.2.cloned.1.call-start = ((), (), s32[]{:S(2)}) async-start(), calls=%async_computation.2 | async-start | bytes 4718592 | tf_op jit(solution)/shard_map/all_gather | solution.py:45
Sparse Core Ops, SparseCore 0:
  130.3 52.3 all-gather.1
where the time goes:
time: 197 us; the launch traced here: 196 us
  waiting for transfers between devices  66.1 us (34%)
  local copies, waits for them, and re-layouts  64.1 us (33%)
  blocking collectives  18.9 us (10%)
  between operations  16.1 us (8%)
  starting transfers between devices  15 us (8%)
  other arithmetic  9.07 us (5%)
  matrix products  6.89 us (3%)
    all_gather x1, waiting for transfers between devices, on_device(): lax.all_gather(at_owner, 'rad', axis=4, tiled=True)  51.1 us
    unnamed x13, local copies, waits for them, and re-layouts  20.9 us
    all_to_all x1, blocking collectives, on_device(): lax.all_to_all(by_degree, 'lat', split_axis=1, concat_axis=0, tiled=True)  18.9 us
    all_to_all x2, local copies, waits for them, and re-layouts, on_device(): lax.all_to_all(picked, 'lat', split_axis=4, concat_axis=5, tiled=True)  17.1 us
    all_to_all x1, waiting for transfers between devices, on_device(): lax.all_to_all(picked, 'lat', split_axis=4, concat_axis=5, tiled=True)  14.9 us
    all_to_all x1, starting transfers between devices, on_device(): lax.all_to_all(picked, 'lat', split_axis=4, concat_axis=5, tiled=True)  14.8 us
    gather x1, local copies, waits for them, and re-layouts, on_device(): by_degree = jnp.take(coefficients, degree_of_slot, axis=1)  8.5 us
    unnamed x1, other arithmetic  5.34 us
  transfers between devices with their start and end apart: 2, of which 2 were waited for; matrix products, arithmetic and copies ran while one was open for 1% of the time, Pallas kernels for 0%

commit v1 on v0

--- a/solution.py
+++ b/solution.py
@@ -42,7 +42,9 @@
     return jnp.einsum(
         "tqfk,mtfck->tqcm",
         matrices,
-        lax.all_gather(at_owner, "rad", axis=4, tiled=True),
+        jnp.concatenate(
+            lax.all_to_all(jnp.stack([at_owner] * lax.axis_size("rad")), "rad", 0, 0), axis=4
+        ),
         preferred_element_type=jnp.float32,
     )
 

time: 197 us -> 212 us (1.076)
  local copies, waits for them, and re-layouts: 64.1 us -> 87.5 us
  between operations: 16.1 us -> 2.72 us
  starting transfers between devices: 15 us -> 21.6 us
  matrix products: 6.89 us -> 4.73 us
    all_gather x1 -> x0, waiting for transfers between devices: 51.1 us -> none  [on_device(): lax.all_gather(at_owner, 'rad', axis=4, tiled=True)]
    all_to_all x0 -> x1, waiting for transfers between devices: none -> 50.4 us  [on_device(): lax.all_to_all(jnp.stack([at_owner] * lax.axis_size('rad')), 'rad', 0, 0)]
    unnamed x13 -> x16, local copies, waits for them, and re-layouts: 20.9 us -> 40 us
    all_to_all x0 -> x1, starting transfers between devices: none -> 6.82 us  [on_device(): lax.all_to_all(jnp.stack([at_owner] * lax.axis_size('rad')), 'rad', 0, 0)]
    reshape x0 -> x2, local copies, waits for them, and re-layouts: none -> 4.34 us  [on_device(): jnp.concatenate(lax.all_to_all(jnp.stack([at_owner] * lax.axis_size('rad'...]
    dot_general x1, matrix products: 4.41 us -> 2.25 us  [on_device(): jnp.einsum('tqfk,mtfck->tqcm', matrices, jnp.concatenate(lax.all_to_all(j...]
    all_to_all x1 -> x0, local copies, waits for them, and re-layouts: 2.16 us -> none  [on_device(): lax.all_to_all(by_degree, 'lat', split_axis=1, concat_axis=0, tiled=True)]
    another operation x0 -> x1, local copies, waits for them, and re-layouts: none -> 2.16 us  [on_device(): jnp.stack([at_owner] * lax.axis_size('rad'))]
where the time goes in v1:
time: 212 us; the launch traced here: 210 us
  local copies, waits for them, and re-layouts  87.5 us (41%)
  waiting for transfers between devices  65.5 us (31%)
  starting transfers between devices  21.6 us (10%)
  blocking collectives  18.9 us (9%)
  other arithmetic  9.07 us (4%)
  matrix products  4.73 us (2%)
  between operations  2.72 us (1%)
    all_to_all x1, waiting for transfers between devices, on_device(): lax.all_to_all(jnp.stack([at_owner] * lax.axis_size('rad')), 'rad', 0, 0)  50.4 us
    unnamed x16, local copies, waits for them, and re-layouts  40 us
    all_to_all x1, blocking collectives, on_device(): lax.all_to_all(by_degree, 'lat', split_axis=1, concat_axis=0, tiled=True)  18.9 us
    all_to_all x2, local copies, waits for them, and re-layouts, on_device(): lax.all_to_all(picked, 'lat', split_axis=4, concat_axis=5, tiled=True)  17.1 us
    all_to_all x1, waiting for transfers between devices, on_device(): lax.all_to_all(picked, 'lat', split_axis=4, concat_axis=5, tiled=True)  15.1 us
    all_to_all x1, starting transfers between devices, on_device(): lax.all_to_all(picked, 'lat', split_axis=4, concat_axis=5, tiled=True)  14.8 us
    gather x1, local copies, waits for them, and re-layouts, on_device(): by_degree = jnp.take(coefficients, degree_of_slot, axis=1)  8.5 us
    all_to_all x1, starting transfers between devices, on_device(): lax.all_to_all(jnp.stack([at_owner] * lax.axis_size('rad')), 'rad', 0, 0)  6.82 us
  transfers between devices with their start and end apart: 2, of which 2 were waited for; matrix products, arithmetic and copies ran while one was open for 1% of the time, Pallas kernels for 0%

profile of v1, /device:TPU:1, one launch (start us, length us, event | category | flops | bytes accessed | tf_op | source)
XLA Modules:
  0.0 210.1 jit_solution(12507287496259405362)
XLA Ops:
  0.0 0.8 compare_select_fusion.1
  0.8 0.7 compare_and_fusion.1
  1.5 7.4 %copy.18 = bf16[2,2,32,2,64,18]{2,5,3,1,0,4:T(8,128)(2,1)} copy(bf16[2,2,32,2,64,18]{4,3,5,2,1,0:T(2,128)(2,1)} %param.6) | data formatting | bytes 1179648 | tf_op args[0]
  8.9 4.5 %gather_fusion = bf16[64,2,2,32,2,18]{3,5,4,2,1,0:T(8,128)(2,1)} fusion(bf16[2,2,32,2,64,18]{2,5,3,1,0,4:T(8,128)(2,1)} %copy.18, s32[1024]{0:T(1024)S(1)} %pad_clamp_fusion), kind=kCustom, calls=%fused_computation | custom fusion | bytes 1179904 | tf_op jit(solution)/shard_map/jit(_take)/gather | solution.py:33
  13.4 2.2 %select_bitcast_fusion = bf16[2,2,32,2,64,18]{2,5,3,1,0,4:T(8,128)(2,1)S(1)} fusion(bf16[64,2,2,32,2,18]{3,5,4,2,1,0:T(8,128)(2,1)} %gather_fusion, pred[64]{0:T(512)(128)(4,1)S(1)} %compare_and_fusion.1), kind=kLoop, calls=%fused_computation.2 | loop fusion | flops 294912 | bytes 1179712 | tf_op jit(solution)/shard_map/jit(_take)/select_n | solution.py:33
  15.6 3.8 %copy.43 = bf16[2,2,32,2,64,18]{2,3,5,1,0,4:T(2,128)(2,1)} copy(bf16[2,2,32,2,64,18]{2,5,3,1,0,4:T(8,128)(2,1)S(1)} %select_bitcast_fusion) | data formatting | bytes 1179648 | tf_op jit(solution)/shard_map/jit(_take)/select_n | solution.py:33
  19.5 6.4 %reshape.158 = bf16[64,2,2304]{2,1,0:T(2,128)(2,1)} reshape(bf16[64,2,2,18,2,32]{5,4,3,2,1,0:T(2,128)(2,1)} %bitcast.72) | data formatting | bytes 1179648
  25.9 14.8 %all-to-all-start = ((bf16[64,2,2304]{2,1,0:T(2,128)(2,1)}), bf16[64,2,2304]{2,1,0:T(2,128)(2,1)S(1)}, u32[]{:S(2)}, u32[]{:S(2)}) async-start(bf16[64,2,2304]{2,1,0:T(2,128)(2,1)} %reshape.158), calls=%async_computation | async-start | bytes 1179648 | tf_op jit(solution)/shard_map/all_to_all | solution.py:34
  43.3 0.7 dynamic-slice.2
  44.7 15.1 %all-to-all-done = bf16[64,2,2304]{2,1,0:T(2,128)(2,1)S(1)} async-done(((bf16[64,2,2304]{2,1,0:T(2,128)(2,1)}), bf16[64,2,2304]{2,1,0:T(2,128)(2,1)S(1)}, u32[]{:S(2)}, u32[]{:S(2)}) %all-to-all-start) | async-done | bytes 589856 | tf_op jit(solution)/shard_map/all_to_all | solution.py:34
  59.7 2.4 %reshape.159 = bf16[64,2,2,18,2,32]{5,4,3,2,1,0:T(2,128)(2,1)} reshape(bf16[64,2,2304]{2,1,0:T(2,128)(2,1)S(1)} %all-to-all-done) | data formatting | bytes 1179648
  62.1 10.1 %copy.20 = bf16[2,2,32,2,64,18]{5,4,2,3,1,0:T(8,128)(2,1)} copy(bf16[2,2,32,2,64,18]{2,3,5,1,0,4:T(2,128)(2,1)} %bitcast.71) | data formatting | bytes 1179648 | tf_op jit(solution)/shard_map/all_to_all | solution.py:34
  72.2 7.0 %all_to_all.9 = bf16[2,2,32,2,1,1152]{5,2,3,1,0,4:T(8,128)(2,1)S(1)} reshape(bf16[2,2,32,2,64,18]{5,4,2,3,1,0:T(8,128)(2,1)} %copy.20) | data formatting | bytes 1179648 | tf_op jit(solution)/shard_map/all_to_all | solution.py:34
  79.2 0.9 fusion
  80.1 1.6 fusion.13
  81.7 2.2 %copy.21 = bf16[1024,2,2,32]{3,2,1,0:T(2,128)(2,1)S(1)} copy(bf16[1024,2,2,32]{0,3,2,1:T(8,128)(2,1)} %fusion.13) | data formatting | bytes 524288 | tf_op jit(solution)/shard_map/convert_element_type | solution.py:24
  83.9 8.5 %gather_fusion.1 = bf16[1024,2,2,32]{3,2,1,0:T(2,128)(2,1)} fusion(bf16[1024,2,2,32]{3,2,1,0:T(2,128)(2,1)S(1)} %copy.21, s32[1024]{0:T(1024)S(1)} %fusion.34), kind=kCustom, calls=%fused_computation.1 | custom fusion | bytes 528384 | tf_op jit(solution)/shard_map/jit(_take)/gather | solution.py:36
  92.4 5.3 %fusion.35 = bf16[1024,1,2,2,32]{4,3,2,1,0:T(2,128)(2,1)S(1)} fusion(bf16[1024,2,2,32]{3,2,1,0:T(2,128)(2,1)} %gather_fusion.1, pred[1024]{0:T(1024)(128)(4,1)S(1)} %compare_and_fusion), kind=kLoop, calls=%fused_computation.44 | loop fusion | flops 131072 | bytes 525312
  97.8 1.7 reshape.160
  99.5 18.9 %all_to_all.26 = bf16[64,2,1024]{2,1,0:T(2,128)(2,1)} all-to-all(bf16[64,2,1024]{2,1,0:T(2,128)(2,1)} %reshape.160), channel_id=1, replica_groups=mesh['lat'=64,'rad'=8] {'lat'}, dimensions={0} | all-to-all | bytes 524288 | tf_op jit(solution)/shard_map/all_to_all | solution.py:37
  118.4 3.0 %reshape.161 = bf16[1024,1,2,2,32]{4,3,2,1,0:T(2,128)(2,1)S(1)} reshape(bf16[64,2,1024]{2,1,0:T(2,128)(2,1)} %all_to_all.26) | data formatting | bytes 524288
  121.4 2.2 %copy.24 = bf16[64,16,2,2,32]{0,4,3,2,1:T(8,128)(2,1)} copy(bf16[64,16,2,2,32]{4,3,2,1,0:T(2,128)(2,1)S(1)} %bitcast.73) | data formatting | bytes 524288 | tf_op jit(solution)/shard_map/stack | solution.py:46
  123.6 4.0 %broadcast_bitcast_fusion = bf16[8,16,2,2,32,64]{5,4,3,2,1,0:T(8,128)(2,1)} fusion(bf16[64,16,2,2,32]{0,4,3,2,1:T(8,128)(2,1)} %copy.24), kind=kLoop, calls=%fused_computation.43 | loop fusion | bytes 2359296
  127.6 7.6 %reshape.162 = bf16[8,2,65536]{2,1,0:T(2,128)(2,1)} reshape(bf16[8,16,2,2,32,64]{5,4,3,2,1,0:T(8,128)(2,1)} %broadcast_bitcast_fusion) | data formatting | bytes 4194304
  135.3 6.8 %all-to-all-start.2 = ((bf16[8,2,65536]{2,1,0:T(2,128)(2,1)}), bf16[8,2,65536]{2,1,0:T(2,128)(2,1)}, u32[]{:S(2)}, u32[]{:S(2)}) async-start(bf16[8,2,65536]{2,1,0:T(2,128)(2,1)} %reshape.162), calls=%async_computation.2 | async-start | bytes 4194304 | tf_op jit(solution)/shard_map/all_to_all | solution.py:46
  142.1 1.3 reshape.106
  143.4 50.4 %all-to-all-done.2 = bf16[8,2,65536]{2,1,0:T(2,128)(2,1)} async-done(((bf16[8,2,65536]{2,1,0:T(2,128)(2,1)}), bf16[8,2,65536]{2,1,0:T(2,128)(2,1)}, u32[]{:S(2)}, u32[]{:S(2)}) %all-to-all-start.2) | async-done | bytes 2097184 | tf_op jit(solution)/shard_map/all_to_all | solution.py:46
  193.8 7.4 %reshape.163 = bf16[8,16,2,2,32,64]{5,4,3,2,1,0:T(8,128)(2,1)} reshape(bf16[8,2,65536]{2,1,0:T(2,128)(2,1)} %all-to-all-done.2) | data formatting | bytes 4194304
  201.2 3.2 %bitcast_bitcast_fusion = bf16[64,16,2,2,8,32]{0,5,3,2,1,4:T(8,128)(2,1)S(1)} fusion(bf16[8,16,2,2,32,64]{5,4,3,2,1,0:T(8,128)(2,1)} %reshape.163), kind=kLoop, calls=%fused_computation.41 | loop fusion | bytes 4194304 | tf_op jit(solution)/shard_map/reshape | solution.py:45
  204.5 1.1 copy.25
  205.6 2.2 %convolution_bitcast_fusion = f32[16,64,2,64]{1,3,2,0:T(8,128)} fusion(bf16[64,16,2,2,256]{0,4,3,2,1:T(8,128)(2,1)S(1)} %bitcast.70, bf16[16,64,2,256,1]{3,2,1,0,4:T(2,128)(2,1)S(1)} %bitcast.74), kind=kOutput, calls=%fused_computation.8 | convolution fusion | flops 134217728 | bytes 3670016 | tf_op jit(solution)/shard_map/tqfk,mtfck->tqcm/dot_general | solution.py:42
  207.8 2.2 %copy.28 = f32[16,64,2,64]{3,2,1,0:T(2,128)} copy(f32[16,64,2,64]{1,3,2,0:T(8,128)} %convolution_bitcast_fusion) | data formatting | bytes 1048576 | tf_op jit(solution)/shard_map/tqfk,mtfck->tqcm/transpose | solution.py:42
  (13 shorter events, 0.7 us)
Async XLA Ops:
  0.0 79.2 %copy-start = (bf16[1,1024,1152]{2,1,0:T(8,128)(2,1)S(1)}, bf16[1,1024,1152]{2,1,0:T(8,128)(2,1)}, u32[]{:S(2)}) copy-start(bf16[1,1024,1152]{2,1,0:T(8,128)(2,1)} %param.7) | copy-start | bytes 7077892
  19.5 21.3 %copy-start.2 = (s32[64]{0:T(128)S(1)}, s32[64]{0:T(128)}, u32[]{:S(2)}) copy-start(s32[64]{0:T(128)} %param.9) | copy-start | bytes 772
  19.5 23.8 %copy-start.3 = (s32[64]{0:T(128)S(1)}, s32[64]{0:T(128)}, u32[]{:S(2)}) copy-start(s32[64]{0:T(128)} %param.11) | copy-start | bytes 772
  19.5 25.2 %copy-start.1 = (s32[1024]{0:T(1024)S(1)}, s32[1024]{0:T(1024)}, u32[]{:S(2)}) copy-start(s32[1024]{0:T(1024)} %param.10) | copy-start | bytes 12292
  25.9 33.8 %all-to-all-start = ((bf16[64,2,2304]{2,1,0:T(2,128)(2,1)}), bf16[64,2,2304]{2,1,0:T(2,128)(2,1)S(1)}, u32[]{:S(2)}, u32[]{:S(2)}) async-start(bf16[64,2,2304]{2,1,0:T(2,128)(2,1)} %reshape.158), calls=%async_computation | async-start | bytes 1179648 | tf_op jit(solution)/shard_map/all_to_all | solution.py:34
  135.3 58.6 %all-to-all-start.2 = ((bf16[8,2,65536]{2,1,0:T(2,128)(2,1)}), bf16[8,2,65536]{2,1,0:T(2,128)(2,1)}, u32[]{:S(2)}, u32[]{:S(2)}) async-start(bf16[8,2,65536]{2,1,0:T(2,128)(2,1)} %reshape.162), calls=%async_computation.2 | async-start | bytes 4194304 | tf_op jit(solution)/shard_map/all_to_all | solution.py:46
